TPU v7x, 32 devices: a whole 2x2x4 slice. The times are simulated.
32 devices in a mesh: blk: 16 (over z, x, core), feat: 2 (over y).
Axes of the slice: x: 2, y: 2, z: 4, core: 2. Of those that a mesh axis runs over, the one named last changes fastest.
Arguments:
- inputs: bfloat16 [4096, 1024], P('blk'), may hold values from -6 to 6
- col_mask: int32 [2, 1024], replicated, may hold values 0 or 1
- row_mask: int32 [4096], P('blk'), may hold values from 0 to 1
- width_class: int32 [4096], P('blk'), may hold values from 0 to 1
- frequencies: bfloat16 [2048, 2048], P(None, 'feat'), may hold values from -0.375 to 0.375
- phases: float32 [2048], P('feat'), may hold values from -3.140625 to 3.140625
- targets: float32 [4096], P('blk'), may hold values from -6 to 6
- prior_draws: float32 [4096, 16], P('blk'), may hold values from -6 to 6
- hidden_weight: float32 [1024, 2048], P('blk', 'feat'), may hold values from -0.1875 to 0.1875
- hidden_moment: float32 [1024, 2048], P('blk', 'feat'), may hold values from -9.536743e-06 to 9.536743e-06
- hidden_second: float32 [1024, 2048], P('blk', 'feat'), may hold values from 4.2e-14 to 1.7e-13
- alpha_weight: float32 [4096, 16], P('blk'), may hold values from -1.5 to 1.5
- alpha_moment: float32 [4096, 16], P('blk'), may hold values from -2.2888184e-05 to 2.2888184e-05
- alpha_second: float32 [4096, 16], P('blk'), may hold values from 1.7578125e-13 to 7.080078e-13
Outputs:
- norm_before: float32 [], replicated
- resid_norm: float32 [], replicated
- hidden_out: float32 [1024, 2048], P('blk', 'feat')
- hidden_moment_out: float32 [1024, 2048], P('blk', 'feat')
- hidden_second_out: float32 [1024, 2048], P('blk', 'feat')
- hidden_copy: bfloat16 [1024, 2048], P('blk', 'feat')
- alpha_out: float32 [4096, 16], P('blk')
- alpha_moment_out: float32 [4096, 16], P('blk')
- alpha_second_out: float32 [4096, 16], P('blk')
- alpha_copy: bfloat16 [4096, 16], P('blk')
All inputs are finite; a program needn't handle non-finite values.
Results may differ from a plain program's by a relative error of at most 0.0034.
Values may be sent and summed in bfloat16 or wider, within the bound.
No kernel may reach another device: no remote copies, remote signals or barrier semaphores. Data moves between devices by JAX's collectives and lax.ppermute only.
A program may use at most 192 MiB of HBM per device.

v0:
```python
import jax
import jax.numpy as jnp
from jax import lax
from jax.sharding import PartitionSpec as P

F = 2048
S = 16
ADAM_STEP = 10
PRECISE = lax.Precision.HIGHEST
NOISE = 0.01
CLIP_AT = 0.01
BETA_ONE = 0.9
BETA_TWO = 0.999
ADAM_EPS = 1e-08
DECAY = 0.01


def adamw_update(weight, moment, second, gradient, step_rate):
    moment = BETA_ONE * moment + (1.0 - BETA_ONE) * gradient
    second = BETA_TWO * second + (1.0 - BETA_TWO) * gradient * gradient
    moment_hat = moment / (1.0 - BETA_ONE**ADAM_STEP)
    second_hat = second / (1.0 - BETA_TWO**ADAM_STEP)
    weight = weight - step_rate * (moment_hat / (jnp.sqrt(second_hat) + ADAM_EPS) + DECAY * weight)
    return (weight, moment, second)


def kernel_step(features, pieces):
    kernel = jnp.einsum("tf,pf->tp", features, pieces[0], preferred_element_type=jnp.float32)
    fitted = jnp.dot(kernel, pieces[1].astype(jnp.float32), precision=PRECISE)
    summed = jnp.einsum("pf,ps->fs", pieces[0], pieces[1], preferred_element_type=jnp.float32)
    return (fitted, summed)


def on_device(
    inputs,
    col_mask,
    row_mask,
    width_class,
    frequencies,
    phases,
    targets,
    prior_draws,
    hidden_weight,
    hidden_moment,
    hidden_second,
    alpha_weight,
    alpha_moment,
    alpha_second,
):
    classes = col_mask.shape[0]
    feat_scale = (2.0 / F) ** 0.5
    onehot = (width_class[:, None] == jnp.arange(classes, dtype=jnp.int32)[None, :]).astype(
        jnp.float32
    )
    keep_cols = jnp.dot(onehot, col_mask.astype(jnp.float32))
    masked = inputs * keep_cols.astype(jnp.bfloat16)
    keep_rows = row_mask.astype(jnp.float32)
    true_count = jnp.maximum(lax.psum(jnp.sum(keep_rows), "blk"), 1.0)
    columns = masked
    first_pre = jnp.dot(
        columns,
        lax.all_gather(hidden_weight.astype(jnp.bfloat16), "blk", axis=0, tiled=True),
        preferred_element_type=jnp.float32,
    )
    tanh_full = jnp.tanh(first_pre)
    hidden = tanh_full.astype(jnp.bfloat16)
    pre = jnp.dot(
        lax.all_gather(hidden, "feat", axis=1, tiled=True),
        frequencies,
        preferred_element_type=jnp.float32,
    )
    phase_arg = pre + phases[None, :]
    features = (feat_scale * jnp.cos(phase_arg)).astype(jnp.bfloat16)
    alpha_low = alpha_weight.astype(jnp.bfloat16)

    def fold_step(pieces):
        return kernel_step(features, pieces)

    fitted_part, moments = fold_step(
        (
            lax.all_gather(features, "blk", axis=0, tiled=True),
            lax.all_gather(alpha_low, "blk", axis=0, tiled=True),
        )
    )
    fitted = lax.psum(fitted_part, "feat") + NOISE * alpha_weight
    residual = fitted - targets[:, None] - prior_draws
    resid_grad = (2.0 * keep_rows[:, None] * residual / (true_count * S)).astype(jnp.bfloat16)
    pulled_part, back_moments = fold_step(
        (
            lax.all_gather(features, "blk", axis=0, tiled=True),
            lax.all_gather(resid_grad, "blk", axis=0, tiled=True),
        )
    )
    alpha_grad = lax.psum(pulled_part, "feat") + NOISE * resid_grad.astype(jnp.float32)
    feature_grad = jnp.dot(resid_grad.astype(jnp.float32), moments.T, precision=PRECISE)
    feature_grad = feature_grad + jnp.dot(
        alpha_low.astype(jnp.float32), back_moments.T, precision=PRECISE
    )
    pre_grad = (-feat_scale * jnp.sin(phase_arg) * feature_grad).astype(jnp.bfloat16)
    hidden_terms = jnp.einsum(
        "tf,hf->th", pre_grad, frequencies, preferred_element_type=jnp.float32
    )
    hidden_grad = lax.psum_scatter(hidden_terms, "feat", scatter_dimension=1, tiled=True)
    first_grad = ((1.0 - tanh_full * tanh_full) * hidden_grad).astype(jnp.bfloat16)
    columns = masked
    weight_grad = lax.psum_scatter(
        jnp.einsum("td,th->dh", columns, first_grad, preferred_element_type=jnp.float32),
        "blk",
        scatter_dimension=0,
        tiled=True,
    )
    first_feat = (lax.axis_index("feat") == 0).astype(jnp.float32)
    grad_part = jnp.sum(weight_grad * weight_grad) + first_feat * jnp.sum(alpha_grad * alpha_grad)
    resid_part = first_feat * jnp.sum(keep_rows[:, None] * residual * residual)
    grad_total, resid_total = lax.psum((grad_part, resid_part), ("blk", "feat"))
    norm_before = jnp.sqrt(grad_total)
    resid_norm = jnp.sqrt(resid_total)
    clip = jnp.minimum(1.0, CLIP_AT / (norm_before + 1e-06))
    hidden_out, moment_out, second_out = adamw_update(
        hidden_weight, hidden_moment, hidden_second, weight_grad * clip, 0.02
    )
    alpha_out, alpha_moment_out, alpha_second_out = adamw_update(
        alpha_weight, alpha_moment, alpha_second, alpha_grad * clip, 0.05
    )
    return (
        norm_before,
        resid_norm,
        hidden_out,
        moment_out,
        second_out,
        hidden_out.astype(jnp.bfloat16),
        alpha_out,
        alpha_moment_out,
        alpha_second_out,
        alpha_out.astype(jnp.bfloat16),
    )


def solution(mesh):
    in_specs = (
        P("blk", None),
        P(),
        P("blk"),
        P("blk"),
        P(None, "feat"),
        P("feat"),
        P("blk"),
        P("blk", None),
        P("blk", "feat"),
        P("blk", "feat"),
        P("blk", "feat"),
        P("blk", None),
        P("blk", None),
        P("blk", None),
    )
    out_specs = (
        P(),
        P(),
        P("blk", "feat"),
        P("blk", "feat"),
        P("blk", "feat"),
        P("blk", "feat"),
        P("blk", None),
        P("blk", None),
        P("blk", None),
        P("blk", None),
    )
    return jax.shard_map(
        on_device, mesh=mesh, in_specs=in_specs, out_specs=out_specs, check_vma=False
    )
```

profile of v0, /device:TPU:0, one launch (start us, length us, event | category | flops | bytes accessed | tf_op | source)
XLA Modules:
  0.0 378.5 jit_solution(18336091625798306020)
XLA Ops:
  7.2 0.0 copy-start.11
  7.2 0.0 all-gather.4.cloned.1.call-start
  7.2 1.6 convert_element_type.47
  8.9 0.0 all-gather.4.cloned.1.call-update
  8.9 0.0 all-gather.6.cloned.1.call-start
  8.9 1.4 fusion.3
  10.3 44.6 %all-gather.4.cloned.1.call-done = bf16[1024,1024]{1,0:T(8,128)(2,1)} async-done(((bf16[64,1024]{1,0:T(8,128)(2,1)}), bf16[1024,1024]{1,0:T(8,128)(2,1)}) %all-gather.4.cloned.1.call-update) | async-done | bytes 2097168 | tf_op jit(solution)/shard_map/all_gather | solution.py:62
  54.9 3.1 fusion.16
  58.1 0.0 all-gather.6.cloned.1.call-update
  58.1 0.0 copy-start.8
  58.1 0.0 copy-start.4
  58.1 0.0 all-gather.8.cloned.1.call-start
  58.2 20.1 %all-gather.6.cloned.1.call-done = bf16[256,2048]{1,0:T(8,128)(2,1)} async-done(((bf16[256,1024]{1,0:T(8,128)(2,1)}), bf16[256,2048]{1,0:T(8,128)(2,1)}) %all-gather.6.cloned.1.call-update) | async-done | bytes 1048592 | tf_op jit(solution)/shard_map/all_gather | solution.py:68
  78.3 0.0 copy-done.11
  78.3 7.3 %multiply_convert_fusion.1 = (bf16[256,1024]{1,0:T(8,128)(2,1)}, f32[256,1024]{1,0:T(8,128)S(1)}) fusion(f32[1024]{0:T(1024)S(1)} %copy-done.11, bf16[256,2048]{1,0:T(8,128)(2,1)} %all-gather.6.cloned.1.call-done, bf16[2048,1024]{1,0:T(8,128)(2,1)} %param.18), kind=kOutput, calls=%fused_computation.9 | convolution fusion | flops 1074528256 | bytes 6819840 | tf_op jit(solution)/shard_map/dot_general | solution.py:67
  85.6 0.0 all-gather.8.cloned.1.call-update
  85.6 0.0 reduce-scatter.3.cloned.1.call-start
  85.6 0.0 copy-done.8
  85.6 0.6 broadcast_multiply_fusion
  86.2 34.6 %psum.36 = f32[]{:T(128)} all-reduce(f32[]{:T(128)} %get-tuple-element.23), channel_id=1, replica_groups=mesh['blk'=16,'feat'=2] {'blk'}, use_global_device_ids=true, to_apply=%region_2.0 | all-reduce | flops 1 | bytes 8 | tf_op jit(solution)/shard_map/psum | solution.py:58
  120.8 0.0 copy-done.4
  121.5 18.8 %all_gather.19 = bf16[4096,16]{0,1:T(8,128)(2,1)S(1)} all-gather(bf16[256,16]{0,1:T(8,128)(2,1)S(1)} %convert_element_type.51), channel_id=1, replica_groups=mesh['blk'=16,'feat'=2] {'blk'}, dimensions={0}, use_global_device_ids=true | all-gather | bytes 139264 | tf_op jit(solution)/shard_map/all_gather | solution.py:82
  140.2 20.7 %all-gather.8.cloned.1.call-done = bf16[4096,1024]{1,0:T(8,128)(2,1)} async-done(((bf16[256,1024]{1,0:T(8,128)(2,1)}), bf16[4096,1024]{1,0:T(8,128)(2,1)}) %all-gather.8.cloned.1.call-update) | async-done | bytes 8388624 | tf_op jit(solution)/shard_map/all_gather | solution.py:81
  160.9 5.9 %fusion.17 = f32[256,4096]{1,0:T(8,128)S(1)} fusion(bf16[256,1024]{1,0:T(8,128)(2,1)} %get-tuple-element.26, bf16[4096,1024]{1,0:T(8,128)(2,1)} %all-gather.8.cloned.1.call-done), kind=kOutput, calls=%fused_computation.36 | convolution fusion | flops 2147483648 | bytes 13107200 | tf_op jit(solution)/shard_map/tf,pf->tp/dot_general | solution.py:28
  166.9 0.0 copy-start
  166.9 1.9 copy-done
  168.8 0.0 copy-start.7
  168.8 0.0 copy-start.9
  168.8 2.0 fusion.18
  170.8 8.3 %psum.35 = f32[256,16]{0,1:T(8,128)S(1)} all-reduce(f32[256,16]{0,1:T(8,128)S(1)} %fusion.18), channel_id=1, replica_groups=mesh['blk'=16,'feat'=2] {'feat'}, use_global_device_ids=true, to_apply=%region_0.0 | all-reduce | flops 4096 | bytes 32768 | tf_op jit(solution)/shard_map/psum | solution.py:85
  179.2 0.0 copy-done.7
  179.2 0.0 copy-done.9
  179.2 0.6 fusion.8
  179.8 19.3 %all_gather.20 = bf16[4096,16]{0,1:T(8,128)(2,1)S(1)} all-gather(bf16[256,16]{0,1:T(8,128)(2,1)S(1)} %divide_convert_fusion), channel_id=1, replica_groups=mesh['blk'=16,'feat'=2] {'blk'}, dimensions={0}, use_global_device_ids=true | all-gather | bytes 139264 | tf_op jit(solution)/shard_map/all_gather | solution.py:91
  199.1 5.8 %fusion.19 = f32[1024,16]{1,0:T(8,128)S(1)} fusion(bf16[4096,1024]{1,0:T(8,128)(2,1)} %all-gather.8.cloned.1.call-done, bf16[4096,16]{0,1:T(8,128)(2,1)S(1)} %all_gather.19), kind=kOutput, calls=%fused_computation.38 | convolution fusion | flops 134217728 | bytes 8585216 | tf_op jit(solution)/shard_map/pf,ps->fs/dot_general | solution.py:30
  204.8 0.6 fusion.20
  205.5 0.0 copy-start.10
  205.5 5.9 %fusion.21 = f32[1024,16]{1,0:T(8,128)S(1)} fusion(bf16[4096,1024]{1,0:T(8,128)(2,1)} %all-gather.8.cloned.1.call-done, bf16[4096,16]{0,1:T(8,128)(2,1)S(1)} %all_gather.20), kind=kOutput, calls=%fused_computation.40 | convolution fusion | flops 134217728 | bytes 8585216 | tf_op jit(solution)/shard_map/pf,ps->fs/dot_general | solution.py:30
  211.4 4.3 %fusion.2 = bf16[256,1024]{1,0:T(8,128)(2,1)S(1)} fusion(f32[256,1024]{1,0:T(8,128)S(1)} %fusion.20, f32[1024,16]{1,0:T(8,128)S(1)} %fusion.21, bf16[256,16]{0,1:T(8,128)(2,1)S(1)} %convert_element_type.51, f32[256,1024]{1,0:T(8,128)S(1)} %get-tuple-element.27), kind=kOutput, calls=%fused_computation.5 | convolution fusion | flops 51380224 | bytes 2695168 | tf_op jit(solution)/shard_map/dot_general | solution.py:96
  215.7 0.0 copy-done.10
  215.7 2.6 fusion.22
  218.3 0.0 reduce-scatter.3.cloned.1.call-update
  218.3 0.0 reduce-scatter.5.cloned.1.call-start
  218.4 28.4 %reduce-scatter.3.cloned.1.call-done = f32[256,1024]{1,0:T(8,128)} async-done(((f32[256,2048]{1,0:T(8,128)}), f32[256,1024]{1,0:T(8,128)}) %reduce-scatter.3.cloned.1.call-update) | async-done | bytes 1048592 | tf_op jit(solution)/shard_map/reduce_scatter | solution.py:103
  246.8 3.9 %fusion.4 = f32[1024,1024]{1,0:T(8,128)} fusion(bf16[256,1024]{1,0:T(8,128)(2,1)S(1)} %fusion.3, f32[256,1024]{1,0:T(8,128)} %reduce-scatter.3.cloned.1.call-done, f32[256,1024]{1,0:T(8,128)S(1)} %get-tuple-element.25), kind=kOutput, calls=%fused_computation.10 | convolution fusion | flops 537919488 | bytes 6815744 | tf_op jit(solution)/shard_map/td,th->dh/dot_general | solution.py:107
  250.8 0.0 copy-start.5
  250.8 0.0 copy-start.6
  250.8 0.0 copy-start.1
  250.8 0.0 copy-start.2
  250.8 0.0 copy-start.3
  250.8 0.0 reduce-scatter.5.cloned.1.call-update
  251.5 4.2 %fusion.23 = f32[256,16]{0,1:T(8,128)S(1)} fusion(f32[256,4096]{1,0:T(8,128)} %copy-done, bf16[4096,16]{0,1:T(8,128)(2,1)S(1)} %all_gather.20), kind=kOutput, calls=%fused_computation.42 | convolution fusion | flops 201326592 | bytes 4341760 | tf_op jit(solution)/shard_map/dot_general | solution.py:29
  255.7 7.0 %psum.37 = f32[256,16]{0,1:T(8,128)S(1)} all-reduce(f32[256,16]{0,1:T(8,128)S(1)} %fusion.23), channel_id=1, replica_groups=mesh['blk'=16,'feat'=2] {'feat'}, use_global_device_ids=true, to_apply=%region_6.0 | all-reduce | flops 4096 | bytes 32768 | tf_op jit(solution)/shard_map/psum | solution.py:94
  262.7 0.6 multiply_reduce_fusion.1
  264.0 59.8 %reduce-scatter.5.cloned.1.call-done = f32[64,1024]{1,0:T(8,128)} async-done(((f32[1024,1024]{1,0:T(8,128)}), f32[64,1024]{1,0:T(8,128)}) %reduce-scatter.5.cloned.1.call-update) | async-done | bytes 262160 | tf_op jit(solution)/shard_map/reduce_scatter | solution.py:106
  323.7 1.6 multiply_reduce_fusion
  326.0 39.6 %all-reduce = (f32[]{:T(128)}, f32[]{:T(128)}) all-reduce(f32[]{:T(128)S(6)} %add.72, f32[]{:T(128)S(6)} %mul.177), channel_id=1, replica_groups=mesh['blk'=16,'feat'=2] {'blk','feat'}, use_global_device_ids=true, to_apply=%region_8.0 | all-reduce | flops 2 | bytes 16 | tf_op jit(solution)/shard_map/psum | solution.py:115
  367.0 0.0 copy-done.5
  367.0 0.0 copy-done.6
  367.0 0.6 fusion.12
  367.7 0.0 copy-done.1
  367.7 0.0 copy-done.2
  367.7 0.0 copy-done.3
  367.7 2.0 fusion.14
  (3 shorter events, 0.0 us)
Async XLA Ops:
  7.2 71.1 %copy-start.11 = (f32[1024]{0:T(1024)S(1)}, f32[1024]{0:T(1024)}, u32[]{:S(2)}) copy-start(f32[1024]{0:T(1024)} %param.19) | copy-start | bytes 12292
  7.2 47.8 %all-gather.4.cloned.1.call-start = ((), (), s32[]{:S(2)}) async-start(), calls=%async_computation.2 | async-start | bytes 2228224 | tf_op jit(solution)/shard_map/all_gather | solution.py:62
  8.9 69.4 %all-gather.6.cloned.1.call-start = ((), (), s32[]{:S(2)}) async-start(), calls=%async_computation.3 | async-start | bytes 1572864 | tf_op jit(solution)/shard_map/all_gather | solution.py:68
  58.1 27.5 %copy-start.8 = (s32[256]{0:T(256)S(1)}, s32[256]{0:T(256)}, u32[]{:S(2)}) copy-start(s32[256]{0:T(256)} %param.16) | copy-start | bytes 3076
  58.1 62.7 %copy-start.4 = (f32[256,16]{0,1:T(8,128)S(1)}, f32[256,16]{0,1:T(8,128)}, u32[]{:S(2)}) copy-start(f32[256,16]{0,1:T(8,128)} %param.25) | copy-start | bytes 49156
  58.1 102.8 %all-gather.8.cloned.1.call-start = ((), (), s32[]{:S(2)}) async-start(), calls=%async_computation.4 | async-start | bytes 8912896 | tf_op jit(solution)/shard_map/all_gather | solution.py:81
  85.6 161.2 %reduce-scatter.3.cloned.1.call-start = ((), (), s32[]{:S(2)}) async-start(), calls=%async_computation.5 | async-start | bytes 3145728 | tf_op jit(solution)/shard_map/reduce_scatter | solution.py:103
  166.9 1.9 copy-start
  168.8 10.3 %copy-start.7 = (f32[256,16]{0,1:T(8,128)S(1)}, f32[256,16]{0,1:T(8,128)}, u32[]{:S(2)}) copy-start(f32[256,16]{0,1:T(8,128)} %param.21) | copy-start | bytes 49156
  168.8 10.3 %copy-start.9 = (f32[256]{0:T(256)S(1)}, f32[256]{0:T(256)}, u32[]{:S(2)}) copy-start(f32[256]{0:T(256)} %param.20) | copy-start | bytes 3076
  205.5 10.2 %copy-start.10 = (bf16[2048,1024]{1,0:T(8,128)(2,1)S(1)}, bf16[2048,1024]{1,0:T(8,128)(2,1)}, u32[]{:S(2)}) copy-start(bf16[2048,1024]{1,0:T(8,128)(2,1)} %param.18) | copy-start | bytes 12582916
  218.3 105.4 %reduce-scatter.5.cloned.1.call-start = ((), (), s32[]{:S(2)}) async-start(), calls=%async_computation.6 | async-start | bytes 4456448 | tf_op jit(solution)/shard_map/reduce_scatter | solution.py:106
  250.8 116.3 %copy-start.5 = (f32[256,16]{0,1:T(8,128)S(1)}, f32[256,16]{0,1:T(8,128)}, u32[]{:S(2)}) copy-start(f32[256,16]{0,1:T(8,128)} %param.26) | copy-start | bytes 49156
  250.8 116.3 %copy-start.6 = (f32[256,16]{0,1:T(8,128)S(1)}, f32[256,16]{0,1:T(8,128)}, u32[]{:S(2)}) copy-start(f32[256,16]{0,1:T(8,128)} %param.27) | copy-start | bytes 49156
  250.8 116.9 %copy-start.1 = (f32[64,1024]{1,0:T(8,128)S(1)}, f32[64,1024]{1,0:T(8,128)}, u32[]{:S(2)}) copy-start(f32[64,1024]{1,0:T(8,128)} %param.22) | copy-start | bytes 786436
  250.8 116.9 %copy-start.2 = (f32[64,1024]{1,0:T(8,128)S(1)}, f32[64,1024]{1,0:T(8,128)}, u32[]{:S(2)}) copy-start(f32[64,1024]{1,0:T(8,128)} %param.23) | copy-start | bytes 786436
  250.8 116.9 %copy-start.3 = (f32[64,1024]{1,0:T(8,128)S(1)}, f32[64,1024]{1,0:T(8,128)}, u32[]{:S(2)}) copy-start(f32[64,1024]{1,0:T(8,128)} %param.24) | copy-start | bytes 786436
Sparse Core Ops, SparseCore 0:
  10.7 44.1 all-gather.3
  58.2 19.9 all-gather.5
  85.7 75.1 all-gather.7
  218.4 28.3 reduce-scatter.2
  250.9 72.7 reduce-scatter.4
where the time goes:
time: 379 us; the launch traced here: 378 us
  waiting for transfers between devices  174 us (46%)
  blocking collectives  128 us (34%)
  matrix products  47.1 us (12%)
  between operations  20.3 us (5%)
  other arithmetic  7.74 us (2%)
    reduce_scatter x1, waiting for transfers between devices, on_device(): lax.psum_scatter(jnp.einsum('td,th->dh', columns, first_grad, preferred_e...  59.8 us
    all_gather x1, waiting for transfers between devices, on_device(): lax.all_gather(hidden_weight.astype(jnp.bfloat16), 'blk', axis=0, tiled=T...  44.6 us
    psum x1, blocking collectives, on_device(): grad_total, resid_total = lax.psum((grad_part, resid_part), ('blk', 'feat'))  39.6 us
    psum x1, blocking collectives, on_device(): true_count = jnp.maximum(lax.psum(jnp.sum(keep_rows), 'blk'), 1.0)  34.6 us
    reduce_scatter x1, waiting for transfers between devices, on_device(): lax.psum_scatter(hidden_terms, 'feat', scatter_dimension=1, tiled=True)  28.4 us
    all_gather x1, waiting for transfers between devices, on_device(): lax.all_gather(features, 'blk', axis=0, tiled=True)  20.7 us
    all_gather x1, waiting for transfers between devices, on_device(): lax.all_gather(hidden, 'feat', axis=1, tiled=True)  20.1 us
    all_gather x1, blocking collectives, on_device(): lax.all_gather(resid_grad, 'blk', axis=0, tiled=True)  19.3 us
  transfers between devices with their start and end apart: 5, of which 5 were waited for; matrix products, arithmetic and copies ran while one was open for 2% of the time, Pallas kernels for 0%

commit v1 on v0

--- a/solution.py
+++ b/solution.py
@@ -13,6 +13,18 @@
 BETA_TWO = 0.999
 ADAM_EPS = 1e-08
 DECAY = 0.01
+
+
+def doubled_up(x, axis, dim):
+    ways, here = (lax.axis_size(axis), lax.axis_index(axis))
+    grown, reach = (x, 1)
+    while reach < ways:
+        theirs = lax.ppermute(grown, axis, [(d, d ^ reach) for d in range(ways)])
+        mine_first = jnp.concatenate([grown, theirs], axis=dim)
+        theirs_first = jnp.concatenate([theirs, grown], axis=dim)
+        grown = jnp.where(here & reach == 0, mine_first, theirs_first)
+        reach = 2 * reach
+    return grown
 
 
 def adamw_update(weight, moment, second, gradient, step_rate):
@@ -86,10 +98,7 @@
     residual = fitted - targets[:, None] - prior_draws
     resid_grad = (2.0 * keep_rows[:, None] * residual / (true_count * S)).astype(jnp.bfloat16)
     pulled_part, back_moments = fold_step(
-        (
-            lax.all_gather(features, "blk", axis=0, tiled=True),
-            lax.all_gather(resid_grad, "blk", axis=0, tiled=True),
-        )
+        (lax.all_gather(features, "blk", axis=0, tiled=True), doubled_up(resid_grad, "blk", 0))
     )
     alpha_grad = lax.psum(pulled_part, "feat") + NOISE * resid_grad.astype(jnp.float32)
     feature_grad = jnp.dot(resid_grad.astype(jnp.float32), moments.T, precision=PRECISE)

time: 379 us -> 373 us (0.984)
  blocking collectives: 128 us -> 108 us
  waiting for transfers between devices: 174 us -> 184 us
    all_gather x1 -> x0, blocking collectives: 19.3 us -> none  [on_device(): lax.all_gather(resid_grad, 'blk', axis=0, tiled=True)]
    ppermute x0 -> x4, waiting for transfers between devices: none -> 9.05 us  [doubled_up(): theirs = lax.ppermute(grown, axis, [(d, d ^ reach) for d in range(ways)])]
  transfers between devices with their start and end apart: 5 -> 9, of which waited for: 5 -> 8; matrix products, arithmetic and copies ran while one was open for 2% -> 4% of each run, Pallas kernels for 0% -> 0%
where the time goes in v1:
time: 373 us; the launch traced here: 372 us
  waiting for transfers between devices  184 us (49%)
  blocking collectives  108 us (29%)
  matrix products  46.9 us (13%)
  between operations  20.3 us (5%)
  other arithmetic  7.78 us (2%)
    reduce_scatter x1, waiting for transfers between devices, on_device(): lax.psum_scatter(jnp.einsum('td,th->dh', columns, first_grad, preferred_e...  59.8 us
    all_gather x1, waiting for transfers between devices, on_device(): lax.all_gather(hidden_weight.astype(jnp.bfloat16), 'blk', axis=0, tiled=T...  44.6 us
    psum x1, blocking collectives, on_device(): grad_total, resid_total = lax.psum((grad_part, resid_part), ('blk', 'feat'))  39.5 us
    psum x1, blocking collectives, on_device(): true_count = jnp.maximum(lax.psum(jnp.sum(keep_rows), 'blk'), 1.0)  34.6 us
    reduce_scatter x1, waiting for transfers between devices, on_device(): lax.psum_scatter(hidden_terms, 'feat', scatter_dimension=1, tiled=True)  29.7 us
    all_gather x1, waiting for transfers between devices, on_device(): lax.all_gather(features, 'blk', axis=0, tiled=True)  20.7 us
    all_gather x1, waiting for transfers between devices, on_device(): lax.all_gather(hidden, 'feat', axis=1, tiled=True)  20.1 us
    all_gather x1, blocking collectives, on_device(): lax.all_gather(alpha_low, 'blk', axis=0, tiled=True)  18.8 us
  transfers between devices with their start and end apart: 9, of which 8 were waited for; matrix products, arithmetic and copies ran while one was open for 4% of the time, Pallas kernels for 0%

profile of v1, /device:TPU:0, one launch (start us, length us, event | category | flops | bytes accessed | tf_op | source)
XLA Modules:
  0.0 372.0 jit_solution(7494557681231112278)
XLA Ops:
  7.2 0.0 copy-start.11
  7.2 0.0 all-gather.4.cloned.1.call-start
  7.2 1.6 convert_element_type.47
  8.9 0.0 all-gather.4.cloned.1.call-update
  8.9 0.0 all-gather.6.cloned.1.call-start
  8.9 1.4 fusion.3
  10.3 44.6 %all-gather.4.cloned.1.call-done = bf16[1024,1024]{1,0:T(8,128)(2,1)} async-done(((bf16[64,1024]{1,0:T(8,128)(2,1)}), bf16[1024,1024]{1,0:T(8,128)(2,1)}) %all-gather.4.cloned.1.call-update) | async-done | bytes 2097168 | tf_op jit(solution)/shard_map/all_gather | solution.py:74
  54.9 3.2 fusion.20
  58.1 0.0 all-gather.6.cloned.1.call-update
  58.1 0.0 copy-start.8
  58.1 0.0 copy-start.4
  58.1 0.0 all-gather.8.cloned.1.call-start
  58.2 20.1 %all-gather.6.cloned.1.call-done = bf16[256,2048]{1,0:T(8,128)(2,1)} async-done(((bf16[256,1024]{1,0:T(8,128)(2,1)}), bf16[256,2048]{1,0:T(8,128)(2,1)}) %all-gather.6.cloned.1.call-update) | async-done | bytes 1048592 | tf_op jit(solution)/shard_map/all_gather | solution.py:80
  78.3 0.0 copy-done.11
  78.3 7.3 %multiply_convert_fusion.1 = (bf16[256,1024]{1,0:T(8,128)(2,1)}, f32[256,1024]{1,0:T(8,128)S(1)}) fusion(f32[1024]{0:T(1024)S(1)} %copy-done.11, bf16[256,2048]{1,0:T(8,128)(2,1)} %all-gather.6.cloned.1.call-done, bf16[2048,1024]{1,0:T(8,128)(2,1)} %param.18), kind=kOutput, calls=%fused_computation.9 | convolution fusion | flops 1074528256 | bytes 6819840 | tf_op jit(solution)/shard_map/dot_general | solution.py:79
  85.6 0.0 all-gather.8.cloned.1.call-update
  85.6 0.0 reduce-scatter.3.cloned.1.call-start
  85.7 0.0 copy-done.8
  85.7 0.6 broadcast_multiply_fusion
  86.3 34.6 %psum.36 = f32[]{:T(128)} all-reduce(f32[]{:T(128)} %get-tuple-element.23), channel_id=1, replica_groups=mesh['blk'=16,'feat'=2] {'blk'}, use_global_device_ids=true, to_apply=%region_2.0 | all-reduce | flops 1 | bytes 8 | tf_op jit(solution)/shard_map/psum | solution.py:70
  120.9 0.0 copy-done.4
  121.5 18.8 %all_gather.16 = bf16[4096,16]{0,1:T(8,128)(2,1)S(1)} all-gather(bf16[256,16]{0,1:T(8,128)(2,1)S(1)} %convert_element_type.51), channel_id=1, replica_groups=mesh['blk'=16,'feat'=2] {'blk'}, dimensions={0}, use_global_device_ids=true | all-gather | bytes 139264 | tf_op jit(solution)/shard_map/all_gather | solution.py:94
  140.3 20.7 %all-gather.8.cloned.1.call-done = bf16[4096,1024]{1,0:T(8,128)(2,1)} async-done(((bf16[256,1024]{1,0:T(8,128)(2,1)}), bf16[4096,1024]{1,0:T(8,128)(2,1)}) %all-gather.8.cloned.1.call-update) | async-done | bytes 8388624 | tf_op jit(solution)/shard_map/all_gather | solution.py:93
  161.0 5.9 %fusion.21 = f32[256,4096]{1,0:T(8,128)S(1)} fusion(bf16[256,1024]{1,0:T(8,128)(2,1)} %get-tuple-element.26, bf16[4096,1024]{1,0:T(8,128)(2,1)} %all-gather.8.cloned.1.call-done), kind=kOutput, calls=%fused_computation.44 | convolution fusion | flops 2147483648 | bytes 13107200 | tf_op jit(solution)/shard_map/tf,pf->tp/dot_general | solution.py:40
  166.9 0.0 copy-start
  166.9 1.9 copy-done
  168.9 2.0 fusion.22
  170.9 8.3 %psum.35 = f32[256,16]{0,1:T(8,128)S(1)} all-reduce(f32[256,16]{0,1:T(8,128)S(1)} %fusion.22), channel_id=1, replica_groups=mesh['blk'=16,'feat'=2] {'feat'}, use_global_device_ids=true, to_apply=%region_0.0 | all-reduce | flops 4096 | bytes 32768 | tf_op jit(solution)/shard_map/psum | solution.py:97
  179.2 0.0 copy-done.7
  179.2 0.0 copy-done.9
  179.2 0.6 fusion.10
  179.8 0.0 collective-permute-start
  179.8 1.2 collective-permute-done
  181.0 0.1 collective-permute-start.1
  181.1 3.6 collective-permute-done.1
  184.8 1.5 collective-permute-start.2
  186.2 5.7 %fusion.23 = f32[1024,16]{1,0:T(8,128)S(1)} fusion(bf16[4096,1024]{1,0:T(8,128)(2,1)} %all-gather.8.cloned.1.call-done, bf16[4096,16]{0,1:T(8,128)(2,1)S(1)} %all_gather.16), kind=kOutput, calls=%fused_computation.46 | convolution fusion | flops 134217728 | bytes 8585216 | tf_op jit(solution)/shard_map/pf,ps->fs/dot_general | solution.py:42
  192.0 0.0 collective-permute-done.2
  192.0 1.0 collective-permute-start.3
  193.1 0.6 fusion.24
  193.7 0.0 copy-start.10
  193.7 4.2 %collective-permute-done.3 = bf16[2048,16]{0,1:T(8,128)(2,1)S(1)} collective-permute-done((bf16[2048,16]{0,1:T(8,128)(2,1)S(1)}, bf16[2048,16]{0,1:T(8,128)(2,1)S(1)}, u32[]{:S(2)}, u32[]{:S(2)}) %collective-permute-start.3) | collective-permute-done | bytes 65568 | tf_op jit(solution)/shard_map/ppermute | solution.py:22
  198.0 5.7 %fusion.9 = f32[1024,16]{1,0:T(8,128)S(1)} fusion(bf16[4096,1024]{1,0:T(8,128)(2,1)} %all-gather.8.cloned.1.call-done, bf16[2048,16]{0,1:T(8,128)(2,1)S(1)} %collective-permute-done.3, bf16[2048,16]{0,1:T(8,128)(2,1)S(1)} %maximum_select_fusion.1, pred[]{:T(512)S(6)} %eq.31), kind=kOutput, calls=%fused_computation.25 | convolution fusion | flops 134807552 | bytes 8585217 | tf_op jit(solution)/shard_map/pf,ps->fs/dot_general | solution.py:42
  203.7 4.3 %fusion.2 = bf16[256,1024]{1,0:T(8,128)(2,1)S(1)} fusion(f32[256,1024]{1,0:T(8,128)S(1)} %fusion.24, f32[1024,16]{1,0:T(8,128)S(1)} %fusion.9, bf16[256,16]{0,1:T(8,128)(2,1)S(1)} %convert_element_type.51, f32[256,1024]{1,0:T(8,128)S(1)} %get-tuple-element.27), kind=kOutput, calls=%fused_computation.5 | convolution fusion | flops 51380224 | bytes 2695168 | tf_op jit(solution)/shard_map/dot_general | solution.py:105
  208.0 0.0 copy-done.10
  208.0 2.6 fusion.25
  210.6 0.0 reduce-scatter.3.cloned.1.call-update
  210.6 0.0 reduce-scatter.5.cloned.1.call-start
  210.7 29.7 %reduce-scatter.3.cloned.1.call-done = f32[256,1024]{1,0:T(8,128)} async-done(((f32[256,2048]{1,0:T(8,128)}), f32[256,1024]{1,0:T(8,128)}) %reduce-scatter.3.cloned.1.call-update) | async-done | bytes 1048592 | tf_op jit(solution)/shard_map/reduce_scatter | solution.py:112
  240.4 3.9 %fusion.4 = f32[1024,1024]{1,0:T(8,128)} fusion(bf16[256,1024]{1,0:T(8,128)(2,1)S(1)} %fusion.3, f32[256,1024]{1,0:T(8,128)} %reduce-scatter.3.cloned.1.call-done, f32[256,1024]{1,0:T(8,128)S(1)} %get-tuple-element.25), kind=kOutput, calls=%fused_computation.10 | convolution fusion | flops 537919488 | bytes 6815744 | tf_op jit(solution)/shard_map/td,th->dh/dot_general | solution.py:116
  244.3 0.0 copy-start.3
  244.3 0.0 reduce-scatter.5.cloned.1.call-update
  245.1 4.2 %fusion.8 = f32[256,16]{0,1:T(8,128)S(1)} fusion(f32[256,4096]{1,0:T(8,128)} %copy-done, bf16[2048,16]{0,1:T(8,128)(2,1)S(1)} %collective-permute-done.3, bf16[2048,16]{0,1:T(8,128)(2,1)S(1)} %maximum_select_fusion.1, pred[]{:T(512)S(6)} %eq.31), kind=kOutput, calls=%fused_computation.24 | convolution fusion | flops 201916416 | bytes 4341761 | tf_op jit(solution)/shard_map/dot_general | solution.py:41
  249.3 7.0 %psum.37 = f32[256,16]{0,1:T(8,128)S(1)} all-reduce(f32[256,16]{0,1:T(8,128)S(1)} %fusion.8), channel_id=1, replica_groups=mesh['blk'=16,'feat'=2] {'feat'}, use_global_device_ids=true, to_apply=%region_6.7 | all-reduce | flops 4096 | bytes 32768 | tf_op jit(solution)/shard_map/psum | solution.py:103
  256.3 0.6 multiply_reduce_fusion.1
  257.5 59.8 %reduce-scatter.5.cloned.1.call-done = f32[64,1024]{1,0:T(8,128)} async-done(((f32[1024,1024]{1,0:T(8,128)}), f32[64,1024]{1,0:T(8,128)}) %reduce-scatter.5.cloned.1.call-update) | async-done | bytes 262160 | tf_op jit(solution)/shard_map/reduce_scatter | solution.py:115
  317.3 1.6 multiply_reduce_fusion
  319.6 39.5 %all-reduce = (f32[]{:T(128)}, f32[]{:T(128)}) all-reduce(f32[]{:T(128)S(6)} %add.72, f32[]{:T(128)S(6)} %mul.177), channel_id=1, replica_groups=mesh['blk'=16,'feat'=2] {'blk','feat'}, use_global_device_ids=true, to_apply=%region_8.9 | all-reduce | flops 2 | bytes 16 | tf_op jit(solution)/shard_map/psum | solution.py:124
  360.6 0.0 copy-done.5
  360.6 0.0 copy-done.6
  360.6 0.6 fusion.16
  361.2 0.0 copy-done.1
  361.2 0.0 copy-done.2
  361.2 2.0 fusion.18
  (13 shorter events, 0.1 us)
Async XLA Ops:
  7.2 71.1 %copy-start.11 = (f32[1024]{0:T(1024)S(1)}, f32[1024]{0:T(1024)}, u32[]{:S(2)}) copy-start(f32[1024]{0:T(1024)} %param.19) | copy-start | bytes 12292
  7.2 47.8 %all-gather.4.cloned.1.call-start = ((), (), s32[]{:S(2)}) async-start(), calls=%async_computation.2 | async-start | bytes 2228224 | tf_op jit(solution)/shard_map/all_gather | solution.py:74
  8.9 69.4 %all-gather.6.cloned.1.call-start = ((), (), s32[]{:S(2)}) async-start(), calls=%async_computation.3 | async-start | bytes 1572864 | tf_op jit(solution)/shard_map/all_gather | solution.py:80
  58.1 27.6 %copy-start.8 = (s32[256]{0:T(256)S(1)}, s32[256]{0:T(256)}, u32[]{:S(2)}) copy-start(s32[256]{0:T(256)} %param.16) | copy-start | bytes 3076
  58.1 62.7 %copy-start.4 = (f32[256,16]{0,1:T(8,128)S(1)}, f32[256,16]{0,1:T(8,128)}, u32[]{:S(2)}) copy-start(f32[256,16]{0,1:T(8,128)} %param.25) | copy-start | bytes 49156
  58.1 102.8 %all-gather.8.cloned.1.call-start = ((), (), s32[]{:S(2)}) async-start(), calls=%async_computation.4 | async-start | bytes 8912896 | tf_op jit(solution)/shard_map/all_gather | solution.py:93
  85.6 154.7 %reduce-scatter.3.cloned.1.call-start = ((), (), s32[]{:S(2)}) async-start(), calls=%async_computation.5 | async-start | bytes 3145728 | tf_op jit(solution)/shard_map/reduce_scatter | solution.py:112
  166.9 2.0 copy-start
  168.9 10.3 %copy-start.7 = (f32[256,16]{0,1:T(8,128)S(1)}, f32[256,16]{0,1:T(8,128)}, u32[]{:S(2)}) copy-start(f32[256,16]{0,1:T(8,128)} %param.21) | copy-start | bytes 49156
  168.9 10.3 %copy-start.9 = (f32[256]{0:T(256)S(1)}, f32[256]{0:T(256)}, u32[]{:S(2)}) copy-start(f32[256]{0:T(256)} %param.20) | copy-start | bytes 3076
  179.8 1.2 collective-permute-start
  181.0 3.7 %collective-permute-start.1 = (bf16[512,16]{0,1:T(8,128)(2,1)S(1)}, bf16[512,16]{0,1:T(8,128)(2,1)S(1)}, u32[]{:S(2)}, u32[]{:S(2)}) collective-permute-start(bf16[512,16]{0,1:T(8,128)(2,1)S(1)} %maximum_select_fusion.5), channel_id=1, source_target_pairs={{0,4},{2,6},{4,0},{6,2},{8,12},{10,14},{12,8},{14,10},{16,20},{18,... | collective-permute-start | bytes 49160 | tf_op jit(solution)/shard_map/ppermute | solution.py:22
  184.8 7.2 %collective-permute-start.2 = (bf16[1024,16]{0,1:T(8,128)(2,1)S(1)}, bf16[1024,16]{0,1:T(8,128)(2,1)S(1)}, u32[]{:S(2)}, u32[]{:S(2)}) collective-permute-start(bf16[1024,16]{0,1:T(8,128)(2,1)S(1)} %maximum_select_fusion.2), channel_id=1, source_target_pairs={{0,8},{2,10},{4,12},{6,14},{8,0},{10,2},{12,4},{14,6},{16,24},{18,... | collective-permute-start | bytes 98312 | tf_op jit(solution)/shard_map/ppermute | solution.py:22
  192.0 5.9 %collective-permute-start.3 = (bf16[2048,16]{0,1:T(8,128)(2,1)S(1)}, bf16[2048,16]{0,1:T(8,128)(2,1)S(1)}, u32[]{:S(2)}, u32[]{:S(2)}) collective-permute-start(bf16[2048,16]{0,1:T(8,128)(2,1)S(1)} %maximum_select_fusion.1), channel_id=1, source_target_pairs={{0,16},{2,18},{4,20},{6,22},{8,24},{10,26},{12,28},{14,30},{16,0},... | collective-permute-start | bytes 196616 | tf_op jit(solution)/shard_map/ppermute | solution.py:22
  193.7 14.3 %copy-start.10 = (bf16[2048,1024]{1,0:T(8,128)(2,1)S(1)}, bf16[2048,1024]{1,0:T(8,128)(2,1)}, u32[]{:S(2)}) copy-start(bf16[2048,1024]{1,0:T(8,128)(2,1)} %param.18) | copy-start | bytes 12582916
  210.6 106.7 %reduce-scatter.5.cloned.1.call-start = ((), (), s32[]{:S(2)}) async-start(), calls=%async_computation.6 | async-start | bytes 4456448 | tf_op jit(solution)/shard_map/reduce_scatter | solution.py:115
  244.3 116.3 %copy-start.5 = (f32[256,16]{0,1:T(8,128)S(1)}, f32[256,16]{0,1:T(8,128)}, u32[]{:S(2)}) copy-start(f32[256,16]{0,1:T(8,128)} %param.26) | copy-start | bytes 49156
  244.3 116.3 %copy-start.6 = (f32[256,16]{0,1:T(8,128)S(1)}, f32[256,16]{0,1:T(8,128)}, u32[]{:S(2)}) copy-start(f32[256,16]{0,1:T(8,128)} %param.27) | copy-start | bytes 49156
  244.3 116.9 %copy-start.1 = (f32[64,1024]{1,0:T(8,128)S(1)}, f32[64,1024]{1,0:T(8,128)}, u32[]{:S(2)}) copy-start(f32[64,1024]{1,0:T(8,128)} %param.22) | copy-start | bytes 786436
  244.3 116.9 %copy-start.2 = (f32[64,1024]{1,0:T(8,128)S(1)}, f32[64,1024]{1,0:T(8,128)}, u32[]{:S(2)}) copy-start(f32[64,1024]{1,0:T(8,128)} %param.23) | copy-start | bytes 786436
  244.3 116.9 %copy-start.3 = (f32[64,1024]{1,0:T(8,128)S(1)}, f32[64,1024]{1,0:T(8,128)}, u32[]{:S(2)}) copy-start(f32[64,1024]{1,0:T(8,128)} %param.24) | copy-start | bytes 786436
Sparse Core Ops, SparseCore 0:
  10.7 44.1 all-gather.3
  58.2 20.0 all-gather.5
  85.7 75.1 all-gather.7
  210.8 29.5 reduce-scatter.2
  244.5 72.8 reduce-scatter.4
